TPU v7x, 32 devices: a whole 2x2x4 slice. The times are simulated.
32 devices in a mesh: groups: 2 (over x), depth: 2 (over core), row: 8 (over z, y).
Axes of the slice: x: 2, y: 2, z: 4, core: 2. Of those that a mesh axis runs over, the one named last changes fastest.
Arguments:
- planes: float32 [4, 4, 512, 512], P('groups', None, 'row'), parts along dimension 0, may hold values from -6 to 6
- slowness: float32 [2, 512, 512], P('depth', 'row'), may hold values from 0.6 to 1.4
- ref_slowness: float32 [2], replicated, may hold values from 0.8 to 1.2
- freq_index: int32 [2], replicated, may hold values from 10 to 51
Outputs:
- image: float32 [4, 512, 512], P(('groups', 'depth'), 'row'), parts along dimension 0
- leaving: float32 [4, 4, 512, 512], P(('groups', 'depth'), None, 'row'), parts along dimension 0
There are 2 independent parts, one for each index of `groups`. A program takes and returns all parts, laid end to end along the dimension named above; an argument that names none is the same for every part. Nothing has to cross between parts.
All inputs are finite; a program needn't handle non-finite values.
Results may differ from a plain program's by a relative error of at most 0.0003.
Values sent between devices are 32-bit elements; how exact they have to be, the bound alone decides.
A program may use at most 64 MiB of HBM per device.

v0:
```python
import functools

import jax
import jax.numpy as jnp
import numpy as np
from jax import lax
from jax.experimental import pallas as pl
from jax.experimental.pallas import tpu as pltpu
from jax.sharding import PartitionSpec as P

OMEGA_STEP = 0.05
DEPTH_STEP = 1.0
MESH = pl.DeviceIdType.MESH
BF16 = jnp.bfloat16
F32 = jnp.float32


def dft_tables(length):
    index = np.arange(length)
    angles = 2.0 * np.pi / length * (index[:, None] * index[None, :] % length)
    parts = []
    for table in (np.cos(angles), np.sin(angles)):
        head = table.astype(BF16)
        parts += [head, (table - head.astype(np.float64)).astype(BF16)]
    return np.stack(parts)


def split(value):
    head = value.astype(BF16)
    return head, (value - head.astype(F32)).astype(BF16)


def dot(a, b):
    return jnp.dot(a, b, preferred_element_type=F32)


def kernel(
    n,
    depth,
    planes_hbm,
    slow_hbm,
    ref_slow,
    freq,
    tables_hbm,
    image_out,
    leaving_out,
    tables,
    fields,
    screens,
    prop,
    phase,
    fsend,
    frecv,
    bsend,
    brecv,
    terms,
    partner_terms,
    load_sem,
    send_sem,
    recv_sem,
    own_sem,
    slow_send,
    slow_recv,
    term_send,
    term_recv,
):
    me = lax.axis_index("row")
    seg = lax.axis_index("depth")
    grid = tables.shape[1]
    rows = grid // n
    cols = rows
    width = fsend.shape[-1]
    kp = width // 2
    freqs = fields.shape[0]
    levels = screens.shape[0]
    own_levels = levels // depth
    order = sorted(range(1, n), key=lambda d: (abs(2 * d - n), d))

    loads = []
    for at, (src, dst) in enumerate(
        [(tables_hbm, tables), (planes_hbm.at[pl.ds(seg * freqs, freqs)], fields)]
    ):
        copy = pltpu.make_async_copy(src, dst, load_sem.at[at])
        copy.start()
        loads.append(copy)
    own_slots = pl.ds(seg * own_levels, own_levels)
    slow_copy = pltpu.make_async_copy(slow_hbm, screens.at[own_slots], load_sem.at[2])
    slow_copy.start()

    barrier = pltpu.get_barrier_semaphore()
    for d in range(1, n):
        pl.semaphore_signal(
            barrier, inc=1, device_id={"row": lax.rem(me + d, n)}, device_id_type=MESH
        )
    for d in range(1, depth):
        pl.semaphore_signal(
            barrier, inc=1, device_id={"depth": lax.rem(seg + d, depth)}, device_id_type=MESH
        )

    def right(value, sign):
        head, tail = split(value)
        count = head.shape[0]
        both = jnp.concatenate([head, tail], axis=0)
        by_cos = dot(both, tables[0])
        by_sin = dot(both, tables[2])
        by_cos = by_cos[:count] + by_cos[count:] + dot(head, tables[1])
        by_sin = by_sin[:count] + by_sin[count:] + dot(head, tables[3])
        half = count // 2
        if sign > 0:
            return by_cos[:half] - by_sin[half:], by_cos[half:] + by_sin[:half]
        return by_cos[:half] + by_sin[half:], by_cos[half:] - by_sin[:half]

    lane = lax.broadcasted_iota(jnp.int32, (1, width), 1)
    lane_sign = jnp.where(lane < kp, 1.0, -1.0).astype(F32)

    def swap(value):
        return pltpu.roll(value, kp, 1) * lane_sign

    def left(value, sign):
        head, tail = split(value)
        turned = swap(value) if sign < 0 else -swap(value)
        turned_head, turned_tail = split(turned)
        by_head = dot(tables[0], jnp.concatenate([head, tail], axis=1)) + dot(
            tables[2], jnp.concatenate([turned_head, turned_tail], axis=1)
        )
        by_tail = dot(tables[1], head) + dot(tables[3], turned_head)
        return by_head[:, :width] + by_head[:, width:] + by_tail

    def exchange(slot, source, target):
        own = pltpu.make_async_copy(source.at[me], target.at[me], own_sem.at[slot])
        own.start()
        copies = [own]
        for d in order:
            to = lax.rem(me + d, n)
            copy = pltpu.make_async_remote_copy(
                src_ref=source.at[to],
                dst_ref=target.at[me],
                send_sem=send_sem.at[slot, d],
                recv_sem=recv_sem.at[slot, d],
                device_id={"row": to},
                device_id_type=MESH,
            )
            copy.start()
            copies.append(copy)
        return copies

    def slot_of(level, stage, f, c):
        return ((level * 2 + stage) * freqs + f) * 2 + c

    def forward(level, f, c):
        both = fields[f, pl.ds(2 * c, 2)].reshape(2 * rows, grid)
        re, im = right(both, -1)
        at = slot_of(level, 0, f, c)
        where = (level * freqs + f) * 2 + c
        for j in range(n):
            block = slice(j * cols, (j + 1) * cols)
            parts = [re[:, block], im[:, block]]
            if cols < kp:
                pad = jnp.zeros((rows, kp - cols), F32)
                parts = [parts[0], pad, parts[1], pad]
            fsend[where, j] = jnp.concatenate(parts, axis=1)
        return exchange(at, fsend.at[where], frecv.at[where])

    def middle(level, f, c):
        where = (level * freqs + f) * 2 + c
        value = left(frecv[where].reshape(grid, width), -1)
        even, odd = prop[level * freqs + f, 0], prop[level * freqs + f, 1]
        turned = swap(value) * odd
        value = value * even + (turned if c == 0 else -turned)
        bsend[where] = left(value, 1).reshape(n, rows, width)
        return exchange(slot_of(level, 1, f, c), bsend.at[where], brecv.at[where])

    def backward(level, f, c):
        where = (level * freqs + f) * 2 + c
        blocks = [brecv[where, i] for i in range(n)]
        re = jnp.concatenate([b[:, :cols] for b in blocks], axis=1)
        im = jnp.concatenate([b[:, kp : kp + cols] for b in blocks], axis=1)
        re, im = right(jnp.concatenate([re, im], axis=0), 1)
        even, odd = phase[level * freqs + f, 0], phase[level * freqs + f, 1]
        if c == 1:
            odd = -odd
        fields[f, 2 * c] = re * even + im * odd
        fields[f, 2 * c + 1] = im * even - re * odd

    def omega_of(f):
        return OMEGA_STEP * freq[seg * freqs + f].astype(F32)

    def signed_wave(positions):
        signed = jnp.where(positions < grid // 2, positions, positions - grid)
        return 2.0 * jnp.pi / grid * signed.astype(F32)

    def propagators(level, f):
        wave_x = signed_wave(lax.broadcasted_iota(jnp.int32, (grid, width), 0))
        at = lax.broadcasted_iota(jnp.int32, (grid, width), 1)
        at = jnp.where(at < kp, at, at - kp)
        wave_y = signed_wave(me * cols + at)
        radicand = (omega_of(f) * ref_slow[level]) ** 2 - (wave_x * wave_x + wave_y * wave_y)
        vertical = jnp.sqrt(jnp.maximum(radicand, 0.0)) * DEPTH_STEP
        damping = jnp.exp(-jnp.sqrt(jnp.maximum(-radicand, 0.0)) * DEPTH_STEP)
        damping = damping * (1.0 / (grid * grid))
        prop[level * freqs + f, 0] = damping * jnp.cos(vertical)
        prop[level * freqs + f, 1] = damping * jnp.sin(vertical)

    def phases(level, f):
        theta = omega_of(f) * (screens[level] - ref_slow[level]) * DEPTH_STEP
        phase[level * freqs + f, 0] = jnp.cos(theta)
        phase[level * freqs + f, 1] = jnp.sin(theta)

    pairs = [(f, c) for f in range(freqs) for c in range(2)]
    pl.semaphore_wait(barrier, n - 1 + depth - 1)
    for copy in loads:
        copy.wait()
    pending = []
    flights = {}
    for f, c in pairs:
        flights[f, c] = forward(0, f, c)
    slow_flights = []
    for d in range(1, depth):
        copy = pltpu.make_async_remote_copy(
            src_ref=slow_hbm,
            dst_ref=screens.at[own_slots],
            send_sem=slow_send.at[d],
            recv_sem=slow_recv.at[d],
            device_id={"depth": lax.rem(seg + d, depth)},
            device_id_type=MESH,
        )
        copy.start()
        slow_flights.append(copy)
    for f in range(freqs):
        propagators(0, f)

    def arrive(copies):
        copies[0].wait()
        for copy in copies[1:]:
            copy.wait_recv()
        pending.extend(copies[1:])

    for level in range(levels):
        returns = {}
        for f, c in pairs:
            arrive(flights[f, c])
            returns[f, c] = middle(level, f, c)
        if level == 0:
            slow_copy.wait()
            for copy in slow_flights:
                copy.wait()
            for f in range(freqs):
                for at in range(levels):
                    phases(at, f)
                    if at > 0:
                        propagators(at, f)
        flights = {}
        for f, c in pairs:
            arrive(returns[f, c])
            backward(level, f, c)
            if level < levels - 1:
                flights[f, c] = forward(level + 1, f, c)
        term = None
        for f in range(freqs):
            part = fields[f, 0] * fields[f, 2] + fields[f, 1] * fields[f, 3]
            term = part if term is None else term + part
        terms[level] = term

    swaps = []
    for d in range(1, depth):
        to = lax.rem(seg + d, depth)
        copy = pltpu.make_async_remote_copy(
            src_ref=terms.at[pl.ds(to * own_levels, own_levels)],
            dst_ref=partner_terms.at[d],
            send_sem=term_send.at[d],
            recv_sem=term_recv.at[d],
            device_id={"depth": to},
            device_id_type=MESH,
        )
        copy.start()
        swaps.append(copy)
    leaving_out[...] = fields[...]
    for copy in pending:
        copy.wait_send()
    for copy in swaps:
        copy.wait()
    total = terms[own_slots]
    for d in range(1, depth):
        total = total + partner_terms[d]
    image_out[...] = total


def shards(n, depth, planes, slowness, ref_slowness, freq_index):
    grid = planes.shape[3]
    rows = grid // n
    freqs = planes.shape[0] // depth
    own_levels = slowness.shape[0]
    levels = own_levels * depth
    kp = max(rows, 64)
    width = 2 * kp
    fields = freqs * 2 * levels
    tables = jnp.asarray(dft_tables(grid))
    any_spec = pl.BlockSpec(memory_space=pl.ANY)
    smem_spec = pl.BlockSpec(memory_space=pltpu.SMEM)
    vmem_spec = pl.BlockSpec(memory_space=pltpu.VMEM)
    blocks = pltpu.VMEM((fields, n, rows, width), F32)
    return pl.pallas_call(
        functools.partial(kernel, n, depth),
        out_shape=(
            jax.ShapeDtypeStruct((own_levels, rows, grid), F32),
            jax.ShapeDtypeStruct((freqs,) + planes.shape[1:], F32),
        ),
        in_specs=[any_spec, any_spec, smem_spec, smem_spec, any_spec],
        out_specs=(vmem_spec, vmem_spec),
        scratch_shapes=[
            pltpu.VMEM(tables.shape, BF16),
            pltpu.VMEM((freqs,) + planes.shape[1:], F32),
            pltpu.VMEM((levels, rows, grid), F32),
            pltpu.VMEM((levels * freqs, 2, grid, width), F32),
            pltpu.VMEM((levels * freqs, 2, rows, grid), F32),
            blocks,
            blocks,
            blocks,
            blocks,
            pltpu.VMEM((levels, rows, grid), F32),
            pltpu.VMEM((depth, own_levels, rows, grid), F32),
            pltpu.SemaphoreType.DMA((3,)),
            pltpu.SemaphoreType.DMA((2 * fields, n)),
            pltpu.SemaphoreType.DMA((2 * fields, n)),
            pltpu.SemaphoreType.DMA((2 * fields,)),
            pltpu.SemaphoreType.DMA((depth,)),
            pltpu.SemaphoreType.DMA((depth,)),
            pltpu.SemaphoreType.DMA((depth,)),
            pltpu.SemaphoreType.DMA((depth,)),
        ],
        compiler_params=pltpu.CompilerParams(
            collective_id=0, has_side_effects=True, vmem_limit_bytes=48 * 1024 * 1024
        ),
    )(planes, slowness, ref_slowness, freq_index, tables)


def solution(mesh):
    in_specs = (P("groups", None, "row", None), P("depth", "row", None), P(), P())
    out_specs = (P(("groups", "depth"), "row", None), P(("groups", "depth"), None, "row", None))
    body = functools.partial(shards, mesh.shape["row"], mesh.shape["depth"])
    return jax.shard_map(body, mesh=mesh, in_specs=in_specs, out_specs=out_specs, check_vma=False)
```

profile of v0, /device:TPU:1, one launch (start us, length us, event | category | flops | bytes accessed | tf_op | source)
XLA Modules:
  0.0 65.4 jit_solution(6977357309913489790)
XLA Ops:
  0.6 0.0 copy-start
  0.6 1.6 %copy-done = bf16[4,512,512]{2,1,0:T(8,128)(2,1)S(1)} copy-done((bf16[4,512,512]{2,1,0:T(8,128)(2,1)S(1)}, bf16[4,512,512]{2,1,0:T(8,128)(2,1)}, u32[]{:S(2)}) %copy-start) | copy-done | bytes 2097176
  2.2 0.0 copy-start.1
  2.2 1.2 %copy-done.1 = f32[2,4,64,512]{3,2,1,0:T(8,128)S(1)} copy-done((f32[2,4,64,512]{3,2,1,0:T(8,128)S(1)}, f32[2,4,64,512]{3,2,1,0:T(8,128)}, u32[]{:S(2)}) %copy-start.1) | copy-done | bytes 1048600
  3.5 0.0 copy-start.2
  3.5 0.9 %copy-done.2 = f32[1,64,512]{2,1,0:T(8,128)S(1)} copy-done((f32[1,64,512]{2,1,0:T(8,128)S(1)}, f32[1,64,512]{2,1,0:T(8,128)}, u32[]{:S(2)}) %copy-start.2) | copy-done | bytes 131096
  4.4 0.0 copy-start.3
  4.4 0.7 copy-done.3
  5.0 0.0 copy-start.4
  5.0 0.7 copy-done.4
  5.7 58.3 %shard_map.68 = (f32[1,64,512]{2,1,0:T(8,128)S(1)}, f32[1,4,64,512]{3,2,1,0:T(8,128)S(1)}) custom-call(f32[2,4,64,512]{3,2,1,0:T(8,128)S(1)} %copy-done.1, f32[1,64,512]{2,1,0:T(8,128)S(1)} %copy-done.2, f32[2]{0:T(128)S(1)} %copy-done.3, s32[2]{0:T(128)S(1)} %copy-done.4, bf16[4,512,512]{2,1,0:T(8,128)(2,1)S(1)} %copy-done), custom_call_target="tpu_custom_call" | custom-call | tf_op jit(solution)/shard_map/pallas_call | solution.py:302
  63.9 0.7 %copy.9 = f32[1,64,512]{2,1,0:T(8,128)} copy(f32[1,64,512]{2,1,0:T(8,128)S(1)} %get-tuple-element.4) | data formatting | bytes 262144
  64.6 0.8 %copy.10 = f32[1,4,64,512]{3,2,1,0:T(8,128)} copy(f32[1,4,64,512]{3,2,1,0:T(8,128)S(1)} %get-tuple-element.5) | data formatting | bytes 1048576
Async XLA Ops:
  0.6 1.6 %copy-start = (bf16[4,512,512]{2,1,0:T(8,128)(2,1)S(1)}, bf16[4,512,512]{2,1,0:T(8,128)(2,1)}, u32[]{:S(2)}) copy-start(bf16[4,512,512]{2,1,0:T(8,128)(2,1)} %constant.2.clone.tables_hbm) | copy-start | bytes 6291460
  2.2 1.2 %copy-start.1 = (f32[2,4,64,512]{3,2,1,0:T(8,128)S(1)}, f32[2,4,64,512]{3,2,1,0:T(8,128)}, u32[]{:S(2)}) copy-start(f32[2,4,64,512]{3,2,1,0:T(8,128)} %planes_hbm.1) | copy-start | bytes 3145732
  3.5 0.9 %copy-start.2 = (f32[1,64,512]{2,1,0:T(8,128)S(1)}, f32[1,64,512]{2,1,0:T(8,128)}, u32[]{:S(2)}) copy-start(f32[1,64,512]{2,1,0:T(8,128)} %slow_hbm.1) | copy-start | bytes 393220
  4.4 0.7 %copy-start.3 = (f32[2]{0:T(128)S(1)}, f32[2]{0:T(128)}, u32[]{:S(2)}) copy-start(f32[2]{0:T(128)} %ref_slow.1) | copy-start | bytes 28
  5.0 0.7 %copy-start.4 = (s32[2]{0:T(128)S(1)}, s32[2]{0:T(128)}, u32[]{:S(2)}) copy-start(s32[2]{0:T(128)} %freq.1) | copy-start | bytes 28
where the time goes:
time: 65.7 us; the launch traced here: 65.4 us
  Pallas kernels  58.3 us (89%)
  local copies, waits for them, and re-layouts  6.47 us (10%)
    pallas_call x1, Pallas kernels, shards(): pl.pallas_call(functools.partial(kernel, n, depth), out_shape=(jax.ShapeD...  58.3 us
    unnamed x12, local copies, waits for them, and re-layouts  6.47 us

commit v1 on v0

v1 whole, which is shorter than its diff:
```python
import functools

import jax
import jax.numpy as jnp
import numpy as np
from jax import lax
from jax.experimental import pallas as pl
from jax.experimental.pallas import tpu as pltpu
from jax.sharding import PartitionSpec as P

OMEGA_STEP = 0.05
DEPTH_STEP = 1.0
MESH = pl.DeviceIdType.MESH
BF16 = jnp.bfloat16
F32 = jnp.float32


def dft_tables(length):
    index = np.arange(length)
    angles = 2.0 * np.pi / length * (index[:, None] * index[None, :] % length)
    parts = []
    for table in (np.cos(angles), np.sin(angles)):
        head = table.astype(BF16)
        parts += [head, (table - head.astype(np.float64)).astype(BF16)]
    return np.stack(parts)


def split(value):
    head = value.astype(BF16)
    return head, (value - head.astype(F32)).astype(BF16)


def dot(a, b):
    return jnp.dot(a, b, preferred_element_type=F32)


def kernel(
    n,
    depth,
    planes_hbm,
    slow_hbm,
    ref_hbm,
    freq_hbm,
    tables_hbm,
    image_out,
    leaving_out,
    ref_slow,
    freq,
    tables,
    fields,
    screens,
    prop,
    phase,
    fsend,
    frecv,
    bsend,
    brecv,
    terms,
    gathered,
    load_sem,
    send_sem,
    recv_sem,
    lone_sem,
    slow_send,
    slow_recv,
    term_send,
    term_recv,
):
    row = lax.axis_index("row")
    seg = lax.axis_index("depth")
    per_band = n // depth
    band = row // per_band
    place = row % per_band * depth + seg
    home = band == seg
    grid = tables.shape[1]
    rows = grid // n
    cols = rows
    width = fsend.shape[-1]
    kp = width // 2
    freqs = fields.shape[0]
    levels = screens.shape[0]
    own_levels = levels // depth
    order = sorted(range(1, n), key=lambda d: (abs(2 * d - n), d))

    loads = []
    wanted = [
        (planes_hbm.at[pl.ds(seg * freqs, freqs)], fields),
        (tables_hbm, tables),
        (ref_hbm, ref_slow),
        (freq_hbm, freq),
    ]
    for at, (src, dst) in enumerate(wanted):
        copy = pltpu.make_async_copy(src, dst, load_sem.at[at])
        copy.start()
        loads.append(copy)

    barrier = pltpu.get_barrier_semaphore()
    for d in range(1, n * depth):
        other = (row * depth + seg + d) % (n * depth)
        pl.semaphore_signal(
            barrier, inc=1, device_id=(lax.axis_index("groups"), other % depth, other // depth),
            device_id_type=MESH,
        )

    pending = []

    def of_row(to_row, to_seg):
        return (lax.axis_index("groups"), to_seg, to_row)

    def member(which, at):
        return of_row(which * per_band + at // depth, at % depth)

    def send(src, dst, send_at, recv_at, device, when, here):
        remote = pltpu.make_async_remote_copy(
            src_ref=src, dst_ref=dst, send_sem=send_at, recv_sem=recv_at,
            device_id=device, device_id_type=MESH,
        )
        local = pltpu.make_async_copy(src, dst, recv_at)
        away = jnp.logical_and(when, jnp.logical_not(here))

        @pl.when(away)
        def _():
            remote.start()

        @pl.when(jnp.logical_and(when, here))
        def _():
            local.start()

        pending.append((remote, away))

    def right(value, sign):
        head, tail = split(value)
        count = head.shape[0]
        both = jnp.concatenate([head, tail], axis=0)
        by_cos = dot(both, tables[0])
        by_sin = dot(both, tables[2])
        by_cos = by_cos[:count] + by_cos[count:] + dot(head, tables[1])
        by_sin = by_sin[:count] + by_sin[count:] + dot(head, tables[3])
        half = count // 2
        if sign > 0:
            return by_cos[:half] - by_sin[half:], by_cos[half:] + by_sin[:half]
        return by_cos[:half] + by_sin[half:], by_cos[half:] - by_sin[:half]

    lane = lax.broadcasted_iota(jnp.int32, (1, width), 1)
    lane_sign = jnp.where(lane < kp, 1.0, -1.0).astype(F32)

    def swap(value):
        return pltpu.roll(value, kp, 1) * lane_sign

    def left(value, sign):
        head, tail = split(value)
        turned = swap(value) if sign < 0 else -swap(value)
        turned_head, turned_tail = split(turned)
        by_head = dot(tables[0], jnp.concatenate([head, tail], axis=1)) + dot(
            tables[2], jnp.concatenate([turned_head, turned_tail], axis=1)
        )
        by_tail = dot(tables[1], head) + dot(tables[3], turned_head)
        return by_head[:, :width] + by_head[:, width:] + by_tail

    def exchange(slot, source, target, device_of, own, here):
        into, index = target
        for d in order:
            to = (own + d) % n
            pltpu.make_async_remote_copy(
                src_ref=source.at[to], dst_ref=into.at[index],
                send_sem=send_sem.at[slot], recv_sem=recv_sem.at[slot],
                device_id=device_of(to), device_id_type=MESH,
            ).start()
        send(
            source.at[own], into.at[index], lone_sem.at[slot], recv_sem.at[slot],
            device_of(own), True, here,
        )
        return slot, source, into

    def arrive(flight):
        slot, _, into = flight
        pltpu.make_async_copy(into, into, recv_sem.at[slot]).wait()
        sent.append(flight)

    def slot_of(level, stage, f, c):
        return ((level * 2 + stage) * freqs + f) * 2 + c

    def forward(level, f, c):
        both = fields[f, pl.ds(2 * c, 2)].reshape(2 * rows, grid)
        re, im = right(both, -1)
        at = slot_of(level, 0, f, c)
        where = (level * freqs + f) * 2 + c
        for j in range(n):
            block = slice(j * cols, (j + 1) * cols)
            parts = [re[:, block], im[:, block]]
            if cols < kp:
                pad = jnp.zeros((rows, kp - cols), F32)
                parts = [parts[0], pad, parts[1], pad]
            fsend[where, j] = jnp.concatenate(parts, axis=1)
        if level == 0:
            return exchange(
                at, fsend.at[where], (frecv.at[where], row), lambda t: member(seg, t), place, home
            )
        return exchange(
            at, fsend.at[where], (frecv.at[where], place), lambda t: member(band, t), place, True
        )

    def middle(level, f, c):
        where = (level * freqs + f) * 2 + c
        value = left(frecv[where].reshape(grid, width), -1)
        even, odd = prop[level * freqs + f, 0], prop[level * freqs + f, 1]
        turned = swap(value) * odd
        value = value * even + (turned if c == 0 else -turned)
        bsend[where] = left(value, 1).reshape(n, rows, width)
        at = slot_of(level, 1, f, c)
        if level == levels - 1:
            return exchange(
                at, bsend.at[where], (brecv.at[where], place), lambda t: of_row(t, band), row, home
            )
        return exchange(
            at, bsend.at[where], (brecv.at[where], place), lambda t: member(band, t), place, True
        )

    def backward(level, f, c):
        where = (level * freqs + f) * 2 + c
        blocks = [brecv[where, i] for i in range(n)]
        re = jnp.concatenate([b[:, :cols] for b in blocks], axis=1)
        im = jnp.concatenate([b[:, kp : kp + cols] for b in blocks], axis=1)
        re, im = right(jnp.concatenate([re, im], axis=0), 1)
        even, odd = phase[level * freqs + f, 0], phase[level * freqs + f, 1]
        if c == 1:
            odd = -odd
        fields[f, 2 * c] = re * even + im * odd
        fields[f, 2 * c + 1] = im * even - re * odd

    def omega_of(segment, f):
        return OMEGA_STEP * freq[segment * freqs + f].astype(F32)

    def signed_wave(positions):
        signed = jnp.where(positions < grid // 2, positions, positions - grid)
        return 2.0 * jnp.pi / grid * signed.astype(F32)

    def propagators(level, f):
        wave_x = signed_wave(lax.broadcasted_iota(jnp.int32, (grid, width), 0))
        at = lax.broadcasted_iota(jnp.int32, (grid, width), 1)
        at = jnp.where(at < kp, at, at - kp)
        wave_y = signed_wave(place * cols + at)
        radicand = (omega_of(band, f) * ref_slow[level]) ** 2 - (wave_x * wave_x + wave_y * wave_y)
        vertical = jnp.sqrt(jnp.maximum(radicand, 0.0)) * DEPTH_STEP
        damping = jnp.exp(-jnp.sqrt(jnp.maximum(-radicand, 0.0)) * DEPTH_STEP)
        damping = damping * (1.0 / (grid * grid))
        prop[level * freqs + f, 0] = damping * jnp.cos(vertical)
        prop[level * freqs + f, 1] = damping * jnp.sin(vertical)

    def phases(level, f):
        theta = omega_of(band if level < levels - 1 else seg, f) * (screens[level] - ref_slow[level]) * DEPTH_STEP
        phase[level * freqs + f, 0] = jnp.cos(theta)
        phase[level * freqs + f, 1] = jnp.sin(theta)

    pairs = [(f, c) for f in range(freqs) for c in range(2)]
    sent = []
    pl.semaphore_wait(barrier, n * depth - 1)
    for level in range(levels):
        owner, at = level // own_levels, level % own_levels
        for k in range(depth):
            if level < levels - 1:
                here = jnp.logical_and(band == k, place == row)
                device = member(k, row)
            else:
                here = seg == k
                device = of_row(row, k)
            send(
                slow_hbm.at[at], screens.at[level], slow_send.at[level, k], slow_recv.at[level],
                device, seg == owner, here,
            )
    flights = {}
    loads[0].wait()
    for copy in loads[1:]:
        copy.wait()
    for f, c in pairs:
        flights[f, c] = forward(0, f, c)
    for f in range(freqs):
        propagators(0, f)

    for level in range(levels):
        returns = {}
        for f, c in pairs:
            arrive(flights[f, c])
            returns[f, c] = middle(level, f, c)
        pltpu.make_async_copy(screens.at[level], screens.at[level], slow_recv.at[level]).wait()
        for f in range(freqs):
            phases(level, f)
            if level < levels - 1:
                propagators(level + 1, f)
        flights = {}
        for f, c in pairs:
            arrive(returns[f, c])
            backward(level, f, c)
            if level < levels - 1:
                flights[f, c] = forward(level + 1, f, c)
        term = None
        for f in range(freqs):
            part = fields[f, 0] * fields[f, 2] + fields[f, 1] * fields[f, 3]
            term = part if term is None else term + part
        terms[level] = term
        owner, at = level // own_levels, level % own_levels
        if level < levels - 1:
            device = of_row(place, owner)
            here = jnp.logical_and(place == row, seg == owner)
            slot = band
        else:
            device = of_row(row, owner)
            here = seg == owner
            slot = seg
        send(
            terms.at[level], gathered.at[at, slot], term_send.at[level], term_recv.at[at],
            device, True, here,
        )

    leaving_out[...] = fields[...]
    for slot, source, _ in sent:
        remote = source.at[pl.ds(0, n - 1)]
        pltpu.make_async_copy(remote, remote, send_sem.at[slot]).wait()
    for at in range(own_levels):
        pltpu.make_async_copy(gathered.at[at], gathered.at[at], term_recv.at[at]).wait()
        total = gathered[at, 0]
        for k in range(1, depth):
            total = total + gathered[at, k]
        image_out[at] = total
    for remote, away in pending:

        @pl.when(away)
        def _(remote=remote):
            remote.wait_send()


def shards(n, depth, planes, slowness, ref_slowness, freq_index):
    grid = planes.shape[3]
    rows = grid // n
    freqs = planes.shape[0] // depth
    own_levels = slowness.shape[0]
    levels = own_levels * depth
    kp = max(rows, 64)
    width = 2 * kp
    fields = freqs * 2 * levels
    tables = jnp.asarray(dft_tables(grid))
    hbm_spec = pl.BlockSpec(memory_space=pltpu.HBM)
    vmem_spec = pl.BlockSpec(memory_space=pltpu.VMEM)
    blocks = pltpu.VMEM((fields, n, rows, width), F32)
    return pl.pallas_call(
        functools.partial(kernel, n, depth),
        out_shape=(
            jax.ShapeDtypeStruct((own_levels, rows, grid), F32),
            jax.ShapeDtypeStruct((freqs,) + planes.shape[1:], F32),
        ),
        in_specs=[hbm_spec] * 5,
        out_specs=(vmem_spec, vmem_spec),
        scratch_shapes=[
            pltpu.SMEM((levels,), F32),
            pltpu.SMEM(freq_index.shape, jnp.int32),
            pltpu.VMEM(tables.shape, BF16),
            pltpu.VMEM((freqs,) + planes.shape[1:], F32),
            pltpu.VMEM((levels, rows, grid), F32),
            pltpu.VMEM((levels * freqs, 2, grid, width), F32),
            pltpu.VMEM((levels * freqs, 2, rows, grid), F32),
            blocks,
            blocks,
            blocks,
            blocks,
            pltpu.VMEM((levels, rows, grid), F32),
            pltpu.VMEM((own_levels, depth, rows, grid), F32),
            pltpu.SemaphoreType.DMA((4,)),
            pltpu.SemaphoreType.DMA((2 * fields,)),
            pltpu.SemaphoreType.DMA((2 * fields,)),
            pltpu.SemaphoreType.DMA((2 * fields,)),
            pltpu.SemaphoreType.DMA((levels, depth)),
            pltpu.SemaphoreType.DMA((levels,)),
            pltpu.SemaphoreType.DMA((levels,)),
            pltpu.SemaphoreType.DMA((own_levels,)),
        ],
        compiler_params=pltpu.CompilerParams(
            collective_id=0, has_side_effects=True, vmem_limit_bytes=48 * 1024 * 1024
        ),
    )(planes, slowness, ref_slowness, freq_index, tables)


def solution(mesh):
    in_specs = (P("groups", None, "row", None), P("depth", "row", None), P(), P())
    out_specs = (P(("groups", "depth"), "row", None), P(("groups", "depth"), None, "row", None))
    body = functools.partial(shards, mesh.shape["row"], mesh.shape["depth"])
    return jax.shard_map(body, mesh=mesh, in_specs=in_specs, out_specs=out_specs, check_vma=False)
```

time: 65.7 us -> 56.2 us (0.86)
  Pallas kernels: 58.3 us -> 48.8 us
    pallas_call x1, Pallas kernels: 58.3 us -> 48.8 us  [shards(): pl.pallas_call(functools.partial(kernel, n, depth), out_shape=(jax.ShapeD...]
where the time goes in v1:
time: 56.2 us; the launch traced here: 55.9 us
  Pallas kernels  48.8 us (87%)
  local copies, waits for them, and re-layouts  6.47 us (12%)
  between operations  0.65 us (1%)
    pallas_call x1, Pallas kernels, shards(): pl.pallas_call(functools.partial(kernel, n, depth), out_shape=(jax.ShapeD...  48.8 us
    unnamed x12, local copies, waits for them, and re-layouts  6.47 us

profile of v1, /device:TPU:1, one launch (start us, length us, event | category | flops | bytes accessed | tf_op | source)
XLA Modules:
  0.0 55.9 jit_solution(17711526808045165989)
XLA Ops:
  0.6 0.0 copy-start
  0.6 1.6 %copy-done = bf16[4,512,512]{2,1,0:T(8,128)(2,1)S(1)} copy-done((bf16[4,512,512]{2,1,0:T(8,128)(2,1)S(1)}, bf16[4,512,512]{2,1,0:T(8,128)(2,1)}, u32[]{:S(2)}) %copy-start) | copy-done | bytes 2097176
  2.2 0.0 copy-start.1
  2.2 1.2 %copy-done.1 = f32[2,4,64,512]{3,2,1,0:T(8,128)S(1)} copy-done((f32[2,4,64,512]{3,2,1,0:T(8,128)S(1)}, f32[2,4,64,512]{3,2,1,0:T(8,128)}, u32[]{:S(2)}) %copy-start.1) | copy-done | bytes 1048600
  3.5 0.0 copy-start.2
  3.5 0.9 %copy-done.2 = f32[1,64,512]{2,1,0:T(8,128)S(1)} copy-done((f32[1,64,512]{2,1,0:T(8,128)S(1)}, f32[1,64,512]{2,1,0:T(8,128)}, u32[]{:S(2)}) %copy-start.2) | copy-done | bytes 131096
  4.4 0.0 copy-start.3
  4.4 0.7 %copy-done.3 = f32[2]{0:T(128)S(1)} copy-done((f32[2]{0:T(128)S(1)}, f32[2]{0:T(128)}, u32[]{:S(2)}) %copy-start.3) | copy-done | bytes 32
  5.0 0.0 copy-start.4
  5.0 0.7 %copy-done.4 = s32[2]{0:T(128)S(1)} copy-done((s32[2]{0:T(128)S(1)}, s32[2]{0:T(128)}, u32[]{:S(2)}) %copy-start.4) | copy-done | bytes 32
  5.7 48.8 %shard_map.68 = (f32[1,64,512]{2,1,0:T(8,128)S(1)}, f32[1,4,64,512]{3,2,1,0:T(8,128)S(1)}) custom-call(f32[2,4,64,512]{3,2,1,0:T(8,128)S(1)} %copy-done.1, f32[1,64,512]{2,1,0:T(8,128)S(1)} %copy-done.2, f32[2]{0:T(128)S(1)} %copy-done.3, s32[2]{0:T(128)S(1)} %copy-done.4, bf16[4,512,512]{2,1,0:T(8,128)(2,1)S(1)} %copy-done), custom_call_target="tpu_custom_call" | custom-call | tf_op jit(solution)/shard_map/pallas_call | solution.py:345
  54.5 0.7 %copy.9 = f32[1,64,512]{2,1,0:T(8,128)} copy(f32[1,64,512]{2,1,0:T(8,128)S(1)} %get-tuple-element.4) | data formatting | bytes 262144
  55.1 0.8 %copy.10 = f32[1,4,64,512]{3,2,1,0:T(8,128)} copy(f32[1,4,64,512]{3,2,1,0:T(8,128)S(1)} %get-tuple-element.5) | data formatting | bytes 1048576
Async XLA Ops:
  0.6 1.6 %copy-start = (bf16[4,512,512]{2,1,0:T(8,128)(2,1)S(1)}, bf16[4,512,512]{2,1,0:T(8,128)(2,1)}, u32[]{:S(2)}) copy-start(bf16[4,512,512]{2,1,0:T(8,128)(2,1)} %constant.2.clone.tables_hbm) | copy-start | bytes 6291460
  2.2 1.2 %copy-start.1 = (f32[2,4,64,512]{3,2,1,0:T(8,128)S(1)}, f32[2,4,64,512]{3,2,1,0:T(8,128)}, u32[]{:S(2)}) copy-start(f32[2,4,64,512]{3,2,1,0:T(8,128)} %planes_hbm.1) | copy-start | bytes 3145732
  3.5 0.9 %copy-start.2 = (f32[1,64,512]{2,1,0:T(8,128)S(1)}, f32[1,64,512]{2,1,0:T(8,128)}, u32[]{:S(2)}) copy-start(f32[1,64,512]{2,1,0:T(8,128)} %slow_hbm.1) | copy-start | bytes 393220
  4.4 0.7 %copy-start.3 = (f32[2]{0:T(128)S(1)}, f32[2]{0:T(128)}, u32[]{:S(2)}) copy-start(f32[2]{0:T(128)} %ref_hbm.1) | copy-start | bytes 28
  5.0 0.7 %copy-start.4 = (s32[2]{0:T(128)S(1)}, s32[2]{0:T(128)}, u32[]{:S(2)}) copy-start(s32[2]{0:T(128)} %freq_hbm.1) | copy-start | bytes 28

commit v2 on v1

--- a/solution.py
+++ b/solution.py
@@ -65,6 +65,7 @@
     slow_recv,
     term_send,
     term_recv,
+    out_sem,
 ):
     row = lax.axis_index("row")
     seg = lax.axis_index("depth")
@@ -268,6 +269,7 @@
                 slow_hbm.at[at], screens.at[level], slow_send.at[level, k], slow_recv.at[level],
                 device, seg == owner, here,
             )
+    leaves = []
     flights = {}
     loads[0].wait()
     for copy in loads[1:]:
@@ -291,7 +293,14 @@
         for f, c in pairs:
             arrive(returns[f, c])
             backward(level, f, c)
-            if level < levels - 1:
+            if level == levels - 1:
+                half = pl.ds(2 * c, 2)
+                copy = pltpu.make_async_copy(
+                    fields.at[f, half], leaving_out.at[f, half], out_sem.at[f, c]
+                )
+                copy.start()
+                leaves.append(copy)
+            else:
                 flights[f, c] = forward(level + 1, f, c)
         term = None
         for f in range(freqs):
@@ -312,7 +321,6 @@
             device, True, here,
         )
 
-    leaving_out[...] = fields[...]
     for slot, source, _ in sent:
         remote = source.at[pl.ds(0, n - 1)]
         pltpu.make_async_copy(remote, remote, send_sem.at[slot]).wait()
@@ -322,6 +330,8 @@
         for k in range(1, depth):
             total = total + gathered[at, k]
         image_out[at] = total
+    for copy in leaves:
+        copy.wait()
     for remote, away in pending:
 
         @pl.when(away)
@@ -349,7 +359,7 @@
             jax.ShapeDtypeStruct((freqs,) + planes.shape[1:], F32),
         ),
         in_specs=[hbm_spec] * 5,
-        out_specs=(vmem_spec, vmem_spec),
+        out_specs=(vmem_spec, hbm_spec),
         scratch_shapes=[
             pltpu.SMEM((levels,), F32),
             pltpu.SMEM(freq_index.shape, jnp.int32),
@@ -372,9 +382,10 @@
             pltpu.SemaphoreType.DMA((levels,)),
             pltpu.SemaphoreType.DMA((levels,)),
             pltpu.SemaphoreType.DMA((own_levels,)),
+            pltpu.SemaphoreType.DMA((freqs, 2)),
         ],
         compiler_params=pltpu.CompilerParams(
-            collective_id=0, has_side_effects=True, vmem_limit_bytes=48 * 1024 * 1024
+            collective_id=0, has_side_effects=True, vmem_limit_bytes=67043328
         ),
     )(planes, slowness, ref_slowness, freq_index, tables)
 

time: 56.2 us -> 53.8 us (0.957)
  local copies, waits for them, and re-layouts: 6.47 us -> 3.44 us
  Pallas kernels: 48.8 us -> 49.6 us
    unnamed x12 -> x2, local copies, waits for them, and re-layouts: 6.47 us -> 3.44 us
    pallas_call x1, Pallas kernels: 48.8 us -> 49.6 us  [shards(): pl.pallas_call(functools.partial(kernel, n, depth), out_shape=(jax.ShapeD...]
where the time goes in v2:
time: 53.8 us; the launch traced here: 53.6 us
  Pallas kernels  49.6 us (92%)
  local copies, waits for them, and re-layouts  3.44 us (6%)
  between operations  0.64 us (1%)
    pallas_call x1, Pallas kernels, shards(): pl.pallas_call(functools.partial(kernel, n, depth), out_shape=(jax.ShapeD...  49.6 us
    unnamed x2, local copies, waits for them, and re-layouts  3.44 us

profile of v2, /device:TPU:1, one launch (start us, length us, event | category | flops | bytes accessed | tf_op | source)
XLA Modules:
  0.0 53.6 jit_solution(585384350399805048)
XLA Ops:
  0.6 49.6 %shard_map.68 = (f32[1,64,512]{2,1,0:T(8,128)}, f32[1,4,64,512]{3,2,1,0:T(8,128)}) custom-call(f32[2,4,64,512]{3,2,1,0:T(8,128)} %planes_hbm.1, f32[1,64,512]{2,1,0:T(8,128)} %slow_hbm.1, f32[2]{0:T(128)} %ref_hbm.1, s32[2]{0:T(128)} %freq_hbm.1, bf16[4,512,512]{2,1,0:T(8,128)(2,1)} %constant.2.clone.tables_hbm), custom_call_target="tpu_custom_call" | custom-call | tf_op jit(solution)/shard_map/pallas_call | solution.py:355
  50.2 1.6 %copy.9 = f32[1,64,512]{2,1,0:T(8,128)} copy(f32[1,64,512]{2,1,0:T(8,128)} %get-tuple-element.4) | data formatting | bytes 262144
  51.8 1.9 %copy.10 = f32[1,4,64,512]{3,2,1,0:T(8,128)} copy(f32[1,4,64,512]{3,2,1,0:T(8,128)} %get-tuple-element.5) | data formatting | bytes 1048576

commit v3 on v2

--- a/solution.py
+++ b/solution.py
@@ -256,6 +256,12 @@
     pairs = [(f, c) for f in range(freqs) for c in range(2)]
     sent = []
     pl.semaphore_wait(barrier, n * depth - 1)
+    leaves = []
+    flights = {}
+    for copy in loads:
+        copy.wait()
+    for f, c in pairs:
+        flights[f, c] = forward(0, f, c)
     for level in range(levels):
         owner, at = level // own_levels, level % own_levels
         for k in range(depth):
@@ -269,13 +275,6 @@
                 slow_hbm.at[at], screens.at[level], slow_send.at[level, k], slow_recv.at[level],
                 device, seg == owner, here,
             )
-    leaves = []
-    flights = {}
-    loads[0].wait()
-    for copy in loads[1:]:
-        copy.wait()
-    for f, c in pairs:
-        flights[f, c] = forward(0, f, c)
     for f in range(freqs):
         propagators(0, f)
 
@@ -355,11 +354,11 @@
     return pl.pallas_call(
         functools.partial(kernel, n, depth),
         out_shape=(
-            jax.ShapeDtypeStruct((own_levels, rows, grid), F32),
-            jax.ShapeDtypeStruct((freqs,) + planes.shape[1:], F32),
+            pltpu.VMEM((own_levels, rows, grid), F32),
+            pltpu.VMEM((freqs,) + planes.shape[1:], F32),
         ),
         in_specs=[hbm_spec] * 5,
-        out_specs=(vmem_spec, hbm_spec),
+        out_specs=(vmem_spec, vmem_spec),
         scratch_shapes=[
             pltpu.SMEM((levels,), F32),
             pltpu.SMEM(freq_index.shape, jnp.int32),
@@ -385,7 +384,7 @@
             pltpu.SemaphoreType.DMA((freqs, 2)),
         ],
         compiler_params=pltpu.CompilerParams(
-            collective_id=0, has_side_effects=True, vmem_limit_bytes=67043328
+            collective_id=0, has_side_effects=True, vmem_limit_bytes=67043328 - (1 << 20)
         ),
     )(planes, slowness, ref_slowness, freq_index, tables)
 

time: 53.8 us -> 52.3 us (0.972)
  local copies, waits for them, and re-layouts: 3.44 us -> 1.45 us
    unnamed x2, local copies, waits for them, and re-layouts: 3.44 us -> 1.45 us
    pallas_call x1, Pallas kernels: 49.6 us -> 50.1 us  [shards(): pl.pallas_call(functools.partial(kernel, n, depth), out_shape=(pltpu.VMEM...]
where the time goes in v3:
time: 52.3 us; the launch traced here: 52.2 us
  Pallas kernels  50.1 us (96%)
  local copies, waits for them, and re-layouts  1.45 us (3%)
  between operations  0.64 us (1%)
    pallas_call x1, Pallas kernels, shards(): pl.pallas_call(functools.partial(kernel, n, depth), out_shape=(pltpu.VMEM...  50.1 us
    unnamed x2, local copies, waits for them, and re-layouts  1.45 us

profile of v3, /device:TPU:1, one launch (start us, length us, event | category | flops | bytes accessed | tf_op | source)
XLA Modules:
  0.0 52.2 jit_solution(16422933341464223728)
XLA Ops:
  0.6 50.1 %shard_map.68 = (f32[1,64,512]{2,1,0:T(8,128)S(1)}, f32[1,4,64,512]{3,2,1,0:T(8,128)S(1)}) custom-call(f32[2,4,64,512]{3,2,1,0:T(8,128)} %planes_hbm.1, f32[1,64,512]{2,1,0:T(8,128)} %slow_hbm.1, f32[2]{0:T(128)} %ref_hbm.1, s32[2]{0:T(128)} %freq_hbm.1, bf16[4,512,512]{2,1,0:T(8,128)(2,1)} %constant.2.clone.tables_hbm), custom_call_target="tpu_custom_call" | custom-call | tf_op jit(solution)/shard_map/pallas_call | solution.py:354
  50.8 0.7 %copy.9 = f32[1,64,512]{2,1,0:T(8,128)} copy(f32[1,64,512]{2,1,0:T(8,128)S(1)} %get-tuple-element.2) | data formatting | bytes 262144
  51.4 0.8 %copy.10 = f32[1,4,64,512]{3,2,1,0:T(8,128)} copy(f32[1,4,64,512]{3,2,1,0:T(8,128)S(1)} %get-tuple-element.3) | data formatting | bytes 1048576

commit v4 on v3

--- a/solution.py
+++ b/solution.py
@@ -81,7 +81,7 @@
     freqs = fields.shape[0]
     levels = screens.shape[0]
     own_levels = levels // depth
-    order = sorted(range(1, n), key=lambda d: (abs(2 * d - n), d))
+    order = range(1, n)
 
     loads = []
     wanted = [
@@ -275,8 +275,9 @@
                 slow_hbm.at[at], screens.at[level], slow_send.at[level, k], slow_recv.at[level],
                 device, seg == owner, here,
             )
-    for f in range(freqs):
-        propagators(0, f)
+    for level in range(levels):
+        for f in range(freqs):
+            propagators(level, f)
 
     for level in range(levels):
         returns = {}
@@ -286,8 +287,6 @@
         pltpu.make_async_copy(screens.at[level], screens.at[level], slow_recv.at[level]).wait()
         for f in range(freqs):
             phases(level, f)
-            if level < levels - 1:
-                propagators(level + 1, f)
         flights = {}
         for f, c in pairs:
             arrive(returns[f, c])

time: 52.3 us -> 49.7 us (0.950)
  the two profiles are of different devices: /device:TPU:1 before, /device:TPU:9 now
where the time goes in v4:
time: 49.7 us; the launch traced here: 49.6 us
  Pallas kernels  47.5 us (96%)
  local copies, waits for them, and re-layouts  1.45 us (3%)
  between operations  0.64 us (1%)
    pallas_call x1, Pallas kernels, shards(): pl.pallas_call(functools.partial(kernel, n, depth), out_shape=(pltpu.VMEM...  47.5 us
    unnamed x2, local copies, waits for them, and re-layouts  1.45 us

profile of v4, /device:TPU:9, one launch (start us, length us, event | category | flops | bytes accessed | tf_op | source)
XLA Modules:
  0.0 49.6 jit_solution(5665336617242338473)
XLA Ops:
  0.6 47.5 %shard_map.68 = (f32[1,64,512]{2,1,0:T(8,128)S(1)}, f32[1,4,64,512]{3,2,1,0:T(8,128)S(1)}) custom-call(f32[2,4,64,512]{3,2,1,0:T(8,128)} %planes_hbm.1, f32[1,64,512]{2,1,0:T(8,128)} %slow_hbm.1, f32[2]{0:T(128)} %ref_hbm.1, s32[2]{0:T(128)} %freq_hbm.1, bf16[4,512,512]{2,1,0:T(8,128)(2,1)} %constant.2.clone.tables_hbm), custom_call_target="tpu_custom_call" | custom-call | tf_op jit(solution)/shard_map/pallas_call | solution.py:353
  48.1 0.7 %copy.9 = f32[1,64,512]{2,1,0:T(8,128)} copy(f32[1,64,512]{2,1,0:T(8,128)S(1)} %get-tuple-element.2) | data formatting | bytes 262144
  48.8 0.8 %copy.10 = f32[1,4,64,512]{3,2,1,0:T(8,128)} copy(f32[1,4,64,512]{3,2,1,0:T(8,128)S(1)} %get-tuple-element.3) | data formatting | bytes 1048576
